TPU v7x, 32 devices: a whole 2x2x4 slice. The times are simulated.
32 devices in a mesh: groups: 1, ctx: 32 (over z, y, x, core).
Axes of the slice: x: 2, y: 2, z: 4, core: 2. Of those that a mesh axis runs over, the one named last changes fastest.
Arguments:
- queries: bfloat16 [8192, 2048], P(('groups', 'ctx')), may hold values from -6 to 6
- keys: bfloat16 [8192, 1024], P(('groups', 'ctx')), may hold values from -6 to 6
- values: bfloat16 [8192, 1024], P(('groups', 'ctx')), may hold values from -6 to 6
- out_grad: bfloat16 [8192, 2048], P(('groups', 'ctx')), may hold values from -96 to 96
- q_gain: float32 [128], replicated, may hold values from 0.25 to 1.75
- k_gain: float32 [128], replicated, may hold values from 0.25 to 1.75
- doc_ids: int32 [128], P(('groups', 'ctx')), may hold values from 0 to 7, never falling along the last dimension, each value on 1 to 48 neighbouring positions
Outputs:
- query_grad: bfloat16 [8192, 2048], P(('groups', 'ctx'))
- key_grad: bfloat16 [8192, 1024], P(('groups', 'ctx'))
- value_grad: bfloat16 [8192, 1024], P(('groups', 'ctx'))
Inputs may be any that keep to these rules, and one draw needn't show every extreme that they name: `doc_ids`: document ids never fall along the sequence; each document covers 1 to 48 whole blocks, and one covers exactly 48.
All inputs are finite; a program needn't handle non-finite values.
Results may differ from a plain program's by a relative error of at most 0.0075.
Values may be sent and summed in bfloat16 or wider, within the bound.
A program may use at most 128 MiB of HBM per device.

v0:
```python
import functools

import jax
import jax.numpy as jnp
from jax import lax
from jax.experimental import pallas as pl
from jax.experimental.pallas import tpu as pltpu
from jax.sharding import PartitionSpec as P

HD = 128
WINDOW = 1024
BLK = 64

qk_scale = 168.0 ** (-0.5)
norm_epsilon = 1e-06

F32 = jnp.float32
BF16 = jnp.bfloat16


def dot(a, b, contract):
    return lax.dot_general(
        a, b, (((contract[0],), (contract[1],)), ((), ())), preferred_element_type=F32
    )


def inverse_rms(x):
    return lax.rsqrt(jnp.mean(x * x, axis=-1, keepdims=True) + norm_epsilon)


def norm_back(x, r, gain, incoming):
    scaled = incoming * gain
    return r * scaled - x * (r * r * r) * jnp.mean(x * scaled, axis=-1, keepdims=True)


def kernel(
    n, q_in, k_in, v_in, g_in, qgain, kgain, docs_in,
    out_q, out_k, out_v,
    qx, gx, kx, docs_own, docs, kv, efar, eown, qn, gn, lsum, osum, drow, dqsum, part0, part2,
    send1, send2, recv1, recv2, dq, dkv,
    x_local, x_send, x_recv, d_sem,
    up_send, up_recv, xn_send, xn_recv,
    g1_send, g1_recv, g2_send, g2_recv,
    fq_local, fq_send, fq_recv, fk_local, fk_send, fk_recv,
):
    T = q_in.shape[0]
    HH = kv.shape[1]
    G = q_in.shape[1] // k_in.shape[1]
    QW = HH * G * HD
    KW = HH * HD
    C = 2 * T
    per = WINDOW // T + 1

    me = lax.axis_index("ctx")
    core = lax.rem(me, 2)
    other = 1 - core
    chip = me // 2
    par = lax.rem(chip, 2)
    partner = me + 1 - 2 * core
    xn = me + 2 - 4 * par
    has_up, has_down = chip < n // 2 - 2, chip >= 2
    up = lax.rem(me + 4, n)
    down = lax.rem(me + n - 4, n)

    barrier = pltpu.get_barrier_semaphore()
    for who in (partner, xn, up, down):
        pl.semaphore_signal(
            barrier, inc=1, device_id={"ctx": who}, device_id_type=pl.DeviceIdType.MESH
        )
    pl.semaphore_wait(barrier, 4)

    def remote(src, dst, s, r, who):
        return pltpu.make_async_remote_copy(
            src_ref=src, dst_ref=dst, send_sem=s, recv_sem=r,
            device_id={"ctx": who}, device_id_type=pl.DeviceIdType.MESH,
        )

    rows = pl.ds(pl.multiple_of(core * T, T), T)
    for b in range(docs_in.shape[0]):
        docs_own[b : b + 1, :] = jnp.full((1, HD), docs_in[b], jnp.int32)

    swaps = []
    rc = remote(docs_own, docs.at[0, core], x_send.at[4], x_recv.at[4], partner)
    lc = pltpu.make_async_copy(docs_own, docs.at[0, core], x_local.at[4])
    rc.start()
    lc.start()
    doc_swap = (rc, lc)

    def swap(src, dst, i, mine, theirs):
        rc = remote(src.at[:, theirs], dst, x_send.at[i], x_recv.at[i], partner)
        rc.start()
        lc = pltpu.make_async_copy(src.at[:, mine], dst, x_local.at[i])
        lc.start()
        return rc, lc

    def part(who, width, at=0, size=None):
        size = width if size is None else size
        return pl.ds(pl.multiple_of(who * width + at, size), size)

    swaps.append(swap(k_in, kx.at[rows, :], 0, part(core, KW), part(other, KW)))
    value_swaps = [
        swap(
            v_in, kv.at[0, h, 1, rows, :], 5 + h,
            part(core, KW, h * HD, HD), part(other, KW, h * HD, HD),
        )
        for h in range(HH)
    ]
    swaps.append(swap(q_in, qx.at[rows, :], 1, part(core, QW), part(other, QW)))
    swaps.append(swap(g_in, gx.at[rows, :], 2, part(core, QW), part(other, QW)))
    swaps.append(doc_swap)
    swaps.extend(value_swaps)

    def arrived(i):
        swaps[i][0].wait_recv()
        swaps[i][1].wait()

    def to_up(h, w):
        return remote(kv.at[0, h, w], kv.at[2, h, w], up_send.at[h, w], up_recv.at[h, w], up)

    def to_xn(slot, h, w):
        return remote(kv.at[slot, h, w], kv.at[1, h, w], xn_send.at[h, w], xn_recv.at[h, w], xn)

    arrived(3)
    doc_up = remote(docs.at[0], docs.at[2], d_sem.at[0], d_sem.at[1], up)

    @pl.when(has_up)
    def _():
        doc_up.start()


    def doc_xn(slot):
        return remote(docs.at[slot], docs.at[1], d_sem.at[2], d_sem.at[3], xn)

    @pl.when(par == 0)
    def _():
        doc_xn(0).start()

    arrived(0)

    for h in range(HH):
        x = kx[:, h * HD : (h + 1) * HD].astype(F32)
        kv[0, h, 0] = (x * inverse_rms(x) * kgain[...]).astype(BF16)
        arrived(4 + h)

        @pl.when(has_up)
        def _():
            for w in range(2):
                to_up(h, w).start()

        if h < HH - 1:

            @pl.when(par == 0)
            def _():
                for w in range(2):
                    to_xn(0, h, w).start()

    @pl.when(chip < 2)
    def _():
        kv[2] = jnp.zeros(kv.shape[1:], BF16)

    @pl.when(chip >= n // 2 - 2)
    def _():
        recv2[...] = jnp.zeros(recv2.shape, BF16)

    @pl.when(has_down)
    def _():
        doc_up.wait_recv()


    @pl.when(par == 1)
    def _():
        doc_xn(2).start()

    doc_xn(0).wait_recv()

    lane = lax.broadcasted_iota(jnp.int32, (1, HD), 1)
    blocks = T // BLK
    qdocs = []
    for m in range(2):
        for b in range(0, blocks, 2):
            qdocs.append(
                jnp.where(lane < BLK, docs[0, m, b : b + 1, :], docs[0, m, b + 1 : b + 2, :])
            )
    lows = []
    for i, qd in enumerate(qdocs):
        low = jnp.zeros((1, HD), jnp.int32)
        for slot in (2, 1, 0):
            for m in range(2):
                for b in range(blocks):
                    kd = jnp.where(chip >= slot, docs[slot, m, b : b + 1, :], -1)
                    low = low + jnp.where(kd < qd, BLK, 0)
        lows.append(jnp.maximum(low, lane + (i * HD + 1)))
    half = len(lows) // 2
    low_rows = [
        jnp.concatenate([x for _ in range(G) for x in lows[t * half : (t + 1) * half]], axis=1)
        for t in range(2)
    ]
    tile_rows = lax.broadcasted_iota(jnp.int32, (T, G * T), 0)
    tile_cols = lax.broadcasted_iota(jnp.int32, (T, G * T), 1)
    causal = tile_rows <= lax.rem(tile_cols, T)

    arrived(1)
    arrived(2)

    def key_tile(h, which, b):
        slot, r = 2 - b // 2, b % 2
        return kv[slot, h, which, r * T : (r + 1) * T, :]

    def take_up(h, w):
        @pl.when(has_down)
        def _():
            to_up(h, w).wait_recv()

        @pl.when(par == 1)
        def _():
            to_xn(2, h, w).start()

    def g1(h, w):
        return remote(
            send1.at[h, w], recv1.at[h, w], g1_send.at[h, w], g1_recv.at[h, w], xn
        )

    def g2(h, w):
        return remote(
            send2.at[h, w], recv2.at[h, w], g2_send.at[h, w], g2_recv.at[h, w], down
        )

    def pass_down(h):
        for w in range(2):
            g1(h, w).wait_recv()

            @pl.when(par == 1)
            def _():
                send2[h, w] = (part2[h, w] + recv1[h, w].astype(F32)).astype(BF16)

            @pl.when((par == 1) & has_down)
            def _():
                g2(h, w).start()

    def fq(h):
        cols = pl.ds(pl.multiple_of(h * (G * HD), G * HD), G * HD)
        to = pl.ds(pl.multiple_of(core * QW + h * (G * HD), G * HD), G * HD)
        return (
            remote(dq.at[other, :, cols], out_q.at[:, to], fq_send.at[h], fq_recv.at[h], partner),
            pltpu.make_async_copy(dq.at[core, :, cols], out_q.at[:, to], fq_local.at[h]),
        )

    def fk(h):
        cols = pl.ds(pl.multiple_of(h * HD, HD), HD)
        to = pl.ds(pl.multiple_of(core * KW + h * HD, HD), HD)
        pairs = []
        for w, out in ((0, out_k), (1, out_v)):
            pairs.append((
                remote(dkv.at[w, other, :, cols], out.at[:, to], fk_send.at[w, h],
                       fk_recv.at[w, h], partner),
                pltpu.make_async_copy(dkv.at[w, core, :, cols], out.at[:, to], fk_local.at[w, h]),
            ))
        return pairs

    qg = qgain[...] * qk_scale
    own_at = {(0, 4): 0, (1, 4): 1, (1, 5): 2}

    def head_cols(h, g):
        return pl.ds(pl.multiple_of((h * G + g) * HD, HD), HD)

    def forward(h, t, b, q):
        s = dot(key_tile(h, 0, b), q, (1, 1))
        seen = tile_rows >= low_rows[t] - b * T
        if b == t + per - 1:
            seen = seen & causal
        e = jnp.where(seen, jnp.exp(s), 0.0)
        eb = e.astype(BF16)
        return eb, jnp.sum(e, axis=0, keepdims=True), dot(key_tile(h, 1, b), eb, (0, 0))

    def backward(h, b, ebs):
        dk = dv = None
        terms = {}
        for t, eb in ebs.items():
            dp = dot(key_tile(h, 1, b), gn[h, t], (1, 1))
            ds = (eb.astype(F32) * (dp - drow[h, t])).astype(BF16)
            dv_t = dot(eb, gn[h, t], (1, 0))
            dk_t = dot(ds, qn[h, t], (1, 0))
            dk = dk_t if dk is None else dk + dk_t
            dv = dv_t if dv is None else dv + dv_t
            terms[t] = dot(key_tile(h, 0, b), ds, (0, 0))
        return dk, dv, terms

    def own_forward(h, carry):
        for t in range(2):
            qn[h, t] = jnp.concatenate(
                [
                    (x * inverse_rms(x) * qg).astype(BF16)
                    for x in (
                        qx[t * T : (t + 1) * T, head_cols(h, g)].astype(F32) for g in range(G)
                    )
                ],
                axis=0,
            )
            total, o_t = 0.0, 0.0
            for b in (4, 5)[: t + 1]:
                eb, part, o_part = forward(h, t, b, qn[h, t])
                eown[h, own_at[t, b]] = eb
                total, o_t = total + part, o_t + o_part
            lsum[h, t] = total
            osum[h, t] = o_t

        for w in range(2):

            @pl.when(h == HH - 2 + w)
            def _():
                take_up(0, w)

        return carry

    lax.fori_loop(0, HH, own_forward, 0)

    def head(h, carry):
        for w in range(2):
            to_xn(0, h, w).wait_recv()
        for t in range(2):
            total, o_t = lsum[h, t], osum[h, t]
            for b in range(t, 4):
                eb, part, o_part = forward(h, t, b, qn[h, t])
                efar[t, b] = eb
                total, o_t = total + part, o_t + o_part
            inv = 1.0 / total
            grads = [gx[t * T : (t + 1) * T, head_cols(h, g)].astype(F32) for g in range(G)]
            g_t = jnp.concatenate(grads, axis=0).T * inv
            drow[h, t] = jnp.sum(g_t.astype(BF16).astype(F32) * o_t, axis=0, keepdims=True) * inv
            gn[h, t] = g_t.T.astype(BF16)

        @pl.when(h + 1 < HH)
        def _():
            take_up(h + 1, 0)

        dq_t = [0.0, 0.0]
        for b in (2, 3):
            dk, dv, terms = backward(h, b, {t: efar[t, b] for t in range(2)})
            at = slice((b - 2) * T, (b - 1) * T)
            send1[h, 0, at] = dk.astype(BF16)
            send1[h, 1, at] = dv.astype(BF16)
            for t in terms:
                dq_t[t] = dq_t[t] + terms[t]
        for w in range(2):
            g1(h, w).start()

        @pl.when((par == 0) & (h == 0))
        def _():
            for w in range(2):
                to_xn(0, HH - 1, w).start()

        @pl.when(h + 1 < HH)
        def _():
            take_up(h + 1, 1)

        for b in (0, 1):
            dk, dv, terms = backward(h, b, {t: efar[t, b] for t in range(b + 1)})
            at = slice(b * T, (b + 1) * T)
            part2[h, 0, at] = dk
            part2[h, 1, at] = dv
            for t in terms:
                dq_t[t] = dq_t[t] + terms[t]
        for t in range(2):
            dqsum[h, t] = dq_t[t]

        @pl.when((par == 0) & has_down)
        def _():
            for w in range(2):
                send2[h, w] = part2[h, w].astype(BF16)
                g2(h, w).start()

        @pl.when(h > 1)
        def _():
            pass_down(h - 2)

        return carry

    lax.fori_loop(0, HH, head, 0)

    def own_backward(h, carry):
        dq_t = [dqsum[h, 0], dqsum[h, 1]]
        for b in (4, 5):
            dk, dv, terms = backward(
                h, b, {t: eown[h, own_at[t, b]] for t in range(b - 4, 2)}
            )
            at = slice((b - 4) * T, (b - 3) * T)
            part0[h, 0, at] = dk
            part0[h, 1, at] = dv
            for t in terms:
                dq_t[t] = dq_t[t] + terms[t]
        for t in range(2):
            dqn = dq_t[t].T
            for g in range(G):
                x = qx[t * T : (t + 1) * T, head_cols(h, g)].astype(F32)
                dq[t, :, head_cols(h, g)] = norm_back(
                    x, inverse_rms(x), qg, dqn[g * T : (g + 1) * T]
                ).astype(BF16)
        far, near = fq(h)
        far.start()
        near.start()

        @pl.when(h == 1)
        def _():
            pass_down(HH - 2)

        return carry

    lax.fori_loop(0, HH, own_backward, 0)
    pass_down(HH - 1)

    def finish(h, carry):
        cols = pl.ds(pl.multiple_of(h * HD, HD), HD)
        @pl.when(has_up)
        def _():
            for w in range(2):
                g2(h, w).wait_recv()

        own = part0[h] + recv2[h].astype(F32)
        own = own + jnp.where(par == 0, recv1[h].astype(F32), 0.0)
        x = kx[:, cols].astype(F32)
        dk = norm_back(x, inverse_rms(x), kgain[...], own[0]).astype(BF16)
        dv = own[1].astype(BF16)
        for m in range(2):
            dkv[0, m, :, cols] = dk[m * T : (m + 1) * T]
            dkv[1, m, :, cols] = dv[m * T : (m + 1) * T]
        for far, near in fk(h):
            far.start()
            near.start()
        return carry

    lax.fori_loop(0, HH, finish, 0)

    for rc, lc in swaps:
        rc.wait_send()

    @pl.when(has_up)
    def _():
        doc_up.wait_send()

    doc_xn(0).wait_send()

    def drain(h, carry):
        for w in range(2):
            to_xn(0, h, w).wait_send()
            g1(h, w).wait_send()

        @pl.when(has_up)
        def _():
            for w in range(2):
                to_up(h, w).wait_send()

        @pl.when(has_down)
        def _():
            for w in range(2):
                g2(h, w).wait_send()

        for far, near in [fq(h)] + fk(h):
            far.wait_send()
            far.wait_recv()
            near.wait()
        return carry

    lax.fori_loop(0, HH, drain, 0)


def on_device(n, queries, keys, values, out_grad, q_gain, k_gain, doc_ids):
    T = queries.shape[0]
    kv_heads = keys.shape[1] // HD
    HH = kv_heads // 2
    G = queries.shape[1] // keys.shape[1]
    C = 2 * T
    per = WINDOW // T + 1
    doc_tile = (-(-doc_ids.shape[0] // 8) * 8, HD)
    DMA = pltpu.SemaphoreType.DMA
    vmem = pl.BlockSpec(memory_space=pltpu.VMEM)
    anywhere = pl.BlockSpec(memory_space=pltpu.HBM)
    scratch = [
        pltpu.VMEM((C, HH * G * HD), BF16),
        pltpu.VMEM((C, HH * G * HD), BF16),
        pltpu.VMEM((C, HH * HD), BF16),
        pltpu.VMEM(doc_tile, jnp.int32),
        pltpu.VMEM((3, 2) + doc_tile, jnp.int32),
        pltpu.VMEM((3, HH, 2, C, HD), BF16),
        pltpu.VMEM((2, per - 1, T, G * T), BF16),
        pltpu.VMEM((HH, 3, T, G * T), BF16),
        pltpu.VMEM((HH, 2, G * T, HD), BF16),
        pltpu.VMEM((HH, 2, G * T, HD), BF16),
        pltpu.VMEM((HH, 2, 1, G * T), F32),
        pltpu.VMEM((HH, 2, HD, G * T), F32),
        pltpu.VMEM((HH, 2, 1, G * T), F32),
        pltpu.VMEM((HH, 2, HD, G * T), F32),
        pltpu.VMEM((HH, 2, C, HD), F32),
        pltpu.VMEM((HH, 2, C, HD), F32),
        pltpu.VMEM((HH, 2, C, HD), BF16),
        pltpu.VMEM((HH, 2, C, HD), BF16),
        pltpu.VMEM((HH, 2, C, HD), BF16),
        pltpu.VMEM((HH, 2, C, HD), BF16),
        pltpu.VMEM((2, T, HH * G * HD), BF16),
        pltpu.VMEM((2, 2, T, HH * HD), BF16),
        DMA((5 + HH,)), DMA((5 + HH,)), DMA((5 + HH,)), DMA((4,)),
        DMA((HH, 2)), DMA((HH, 2)), DMA((HH, 2)), DMA((HH, 2)),
        DMA((HH, 2)), DMA((HH, 2)), DMA((HH, 2)), DMA((HH, 2)),
        DMA((HH,)), DMA((HH,)), DMA((HH,)), DMA((2, HH)), DMA((2, HH)), DMA((2, HH)),
    ]
    return pl.pallas_call(
        functools.partial(kernel, n),
        out_shape=(
            pltpu.VMEM(queries.shape, BF16),
            pltpu.VMEM(keys.shape, BF16),
            pltpu.VMEM(values.shape, BF16),
        ),
        in_specs=[anywhere] * 4 + [vmem, vmem, pl.BlockSpec(memory_space=pltpu.SMEM)],
        out_specs=(vmem, vmem, vmem),
        scratch_shapes=scratch,
        compiler_params=pltpu.CompilerParams(
            collective_id=0, has_side_effects=True, vmem_limit_bytes=64700000
        ),
    )(queries, keys, values, out_grad, q_gain.reshape(1, HD), k_gain.reshape(1, HD), doc_ids)


def solution(mesh):
    split = P(("groups", "ctx"), None)
    return jax.shard_map(
        functools.partial(on_device, mesh.shape["ctx"]),
        mesh=mesh,
        in_specs=(split, split, split, split, P(), P(), P(("groups", "ctx"))),
        out_specs=(split, split, split),
        check_vma=False,
    )
```

profile of v0, /device:TPU:3, one launch (start us, length us, event | category | flops | bytes accessed | tf_op | source)
XLA Modules:
  0.0 74.8 jit_solution(10192100710298489302)
XLA Ops:
  0.6 71.6 %shard_map.94 = (bf16[256,2048]{1,0:T(8,128)(2,1)S(1)}, bf16[256,1024]{1,0:T(8,128)(2,1)S(1)}, bf16[256,1024]{1,0:T(8,128)(2,1)S(1)}) custom-call(bf16[256,2048]{1,0:T(8,128)(2,1)} %q_in.1, bf16[256,1024]{1,0:T(8,128)(2,1)} %k_in.1, bf16[256,1024]{1,0:T(8,128)(2,1)} %v_in.1, bf16[256,2048]{1,0:T(8,128)(2,1)} %g_in.1, f32[1,128]{1,0:T(1,128)} %bitcast.2, ...), custom_call_target="tpu_custom_call" | custom-call | tf_op jit(solution)/shard_map/pallas_call | solution.py:505
  72.3 1.0 %copy.13 = bf16[256,2048]{1,0:T(8,128)(2,1)} copy(bf16[256,2048]{1,0:T(8,128)(2,1)S(1)} %get-tuple-element.3) | data formatting | bytes 2097152
  73.3 0.8 %copy.14 = bf16[256,1024]{1,0:T(8,128)(2,1)} copy(bf16[256,1024]{1,0:T(8,128)(2,1)S(1)} %get-tuple-element.4) | data formatting | bytes 1048576
  74.1 0.8 %copy.15 = bf16[256,1024]{1,0:T(8,128)(2,1)} copy(bf16[256,1024]{1,0:T(8,128)(2,1)S(1)} %get-tuple-element.5) | data formatting | bytes 1048576
where the time goes:
time: 75 us; the launch traced here: 74.8 us
  Pallas kernels  71.6 us (95%)
  local copies, waits for them, and re-layouts  2.56 us (3%)
    pallas_call x1, Pallas kernels, on_device(): pl.pallas_call(functools.partial(kernel, n), out_shape=(pltpu.VMEM(querie...  71.6 us
    unnamed x3, local copies, waits for them, and re-layouts  2.56 us

commit v1 on v0

--- a/solution.py
+++ b/solution.py
@@ -36,9 +36,9 @@
 def kernel(
     n, q_in, k_in, v_in, g_in, qgain, kgain, docs_in,
     out_q, out_k, out_v,
-    qx, gx, kx, docs_own, docs, kv, efar, eown, qn, gn, lsum, osum, drow, dqsum, part0, part2,
+    qx, gx, kx, docs_own, docs, kv, kn, efar, eown, qn, gn, lsum, osum, drow, dqsum, part0, part2,
     send1, send2, recv1, recv2, dq, dkv,
-    x_local, x_send, x_recv, d_sem,
+    x_local, x_send, x_recv, du_send, du_recv, dx_send, dx_recv,
     up_send, up_recv, xn_send, xn_recv,
     g1_send, g1_recv, g2_send, g2_recv,
     fq_local, fq_send, fq_recv, fk_local, fk_send, fk_recv,
@@ -63,11 +63,11 @@
     down = lax.rem(me + n - 4, n)
 
     barrier = pltpu.get_barrier_semaphore()
-    for who in (partner, xn, up, down):
+    flip = 1 - 2 * core
+    for who in (partner, xn, xn + flip, up, up + flip, down, down + flip):
         pl.semaphore_signal(
             barrier, inc=1, device_id={"ctx": who}, device_id_type=pl.DeviceIdType.MESH
         )
-    pl.semaphore_wait(barrier, 4)
 
     def remote(src, dst, s, r, who):
         return pltpu.make_async_remote_copy(
@@ -75,103 +75,138 @@
             device_id={"ctx": who}, device_id_type=pl.DeviceIdType.MESH,
         )
 
-    rows = pl.ds(pl.multiple_of(core * T, T), T)
+    def half(c):
+        return pl.ds(pl.multiple_of(c * T, T), T)
+
+    rows = half(core)
     for b in range(docs_in.shape[0]):
         docs_own[b : b + 1, :] = jnp.full((1, HD), docs_in[b], jnp.int32)
-
-    swaps = []
-    rc = remote(docs_own, docs.at[0, core], x_send.at[4], x_recv.at[4], partner)
-    lc = pltpu.make_async_copy(docs_own, docs.at[0, core], x_local.at[4])
-    rc.start()
-    lc.start()
-    doc_swap = (rc, lc)
-
-    def swap(src, dst, i, mine, theirs):
-        rc = remote(src.at[:, theirs], dst, x_send.at[i], x_recv.at[i], partner)
-        rc.start()
-        lc = pltpu.make_async_copy(src.at[:, mine], dst, x_local.at[i])
-        lc.start()
-        return rc, lc
 
     def part(who, width, at=0, size=None):
         size = width if size is None else size
         return pl.ds(pl.multiple_of(who * width + at, size), size)
 
-    swaps.append(swap(k_in, kx.at[rows, :], 0, part(core, KW), part(other, KW)))
-    value_swaps = [
+    def swap(src, dst, i, mine, theirs):
+        rc = remote(src.at[:, theirs], dst, x_send.at[i], x_recv.at[i], partner)
+        lc = pltpu.make_async_copy(src.at[:, mine], dst, x_local.at[i])
+        return rc, lc
+
+    swaps = [
+        swap(k_in, kx.at[rows, :], 0, part(core, KW), part(other, KW)),
+        swap(q_in, qx.at[rows, :], 1, part(core, QW), part(other, QW)),
+        swap(g_in, gx.at[rows, :], 2, part(core, QW), part(other, QW)),
+        (
+            remote(docs_own, docs.at[0, core], x_send.at[3], x_recv.at[3], partner),
+            pltpu.make_async_copy(docs_own, docs.at[0, core], x_local.at[3]),
+        ),
+    ] + [
         swap(
-            v_in, kv.at[0, h, 1, rows, :], 5 + h,
+            v_in, kv.at[0, h, 1, rows, :], 4 + h,
             part(core, KW, h * HD, HD), part(other, KW, h * HD, HD),
         )
         for h in range(HH)
     ]
-    swaps.append(swap(q_in, qx.at[rows, :], 1, part(core, QW), part(other, QW)))
-    swaps.append(swap(g_in, gx.at[rows, :], 2, part(core, QW), part(other, QW)))
-    swaps.append(doc_swap)
-    swaps.extend(value_swaps)
+    order = (3, 0, 4, 1, 5, 6, 7, 2) if HH == 4 else tuple(range(len(swaps)))
 
     def arrived(i):
         swaps[i][0].wait_recv()
         swaps[i][1].wait()
 
-    def to_up(h, w):
-        return remote(kv.at[0, h, w], kv.at[2, h, w], up_send.at[h, w], up_recv.at[h, w], up)
-
-    def to_xn(slot, h, w):
-        return remote(kv.at[slot, h, w], kv.at[1, h, w], xn_send.at[h, w], xn_recv.at[h, w], xn)
-
-    arrived(3)
-    doc_up = remote(docs.at[0], docs.at[2], d_sem.at[0], d_sem.at[1], up)
+    def reach(who, c):
+        return who + (c - core)
+
+    def to_up(h, w, j, s):
+        src = (k_in, v_in)[w].at[:, part(j, KW, h * HD, HD)]
+        return remote(
+            src, kv.at[2, h, w, half(s), :], up_send.at[h, w, j], up_recv.at[h, w, s],
+            reach(up, j),
+        )
+
+    def to_xn(h, w, j, s):
+        src = (k_in, v_in)[w].at[:, part(j, KW, h * HD, HD)]
+        return remote(
+            src, kv.at[1, h, w, half(s), :], xn_send.at[h, w, j], xn_recv.at[h, w, s],
+            reach(xn, j),
+        )
+
+    def relay(h, w, s):
+        return remote(
+            kv.at[2, h, w, half(s), :], kv.at[1, h, w, half(s), :],
+            xn_send.at[h, w, s], xn_recv.at[h, w, s], xn,
+        )
+
+    def doc_up(j, s):
+        return remote(docs_own, docs.at[2, s], du_send.at[j], du_recv.at[s], reach(up, j))
+
+    def doc_xn(j, s):
+        return remote(docs_own, docs.at[1, s], dx_send.at[j], dx_recv.at[s], reach(xn, j))
+
+    def doc_relay(s):
+        return remote(docs.at[2, s], docs.at[1, s], dx_send.at[s], dx_recv.at[s], xn)
+
+    for i in order:
+        swaps[i][1].start()
+
+    pl.semaphore_wait(barrier, 7)
+
+    both = (core, other)
+    swaps[3][0].start()
 
     @pl.when(has_up)
     def _():
-        doc_up.start()
-
-
-    def doc_xn(slot):
-        return remote(docs.at[slot], docs.at[1], d_sem.at[2], d_sem.at[3], xn)
+        for j in both:
+            doc_up(j, core).start()
 
     @pl.when(par == 0)
     def _():
-        doc_xn(0).start()
+        for j in both:
+            doc_xn(j, core).start()
+
+    for h in range(HH):
+
+        @pl.when(has_up)
+        def _():
+            for w in range(2):
+                for j in both:
+                    to_up(h, w, j, core).start()
+
+        @pl.when(par == 0)
+        def _():
+            for w in range(2):
+                for j in both:
+                    to_xn(h, w, j, core).start()
+
+    for i in order[1:]:
+        swaps[i][0].start()
+
+    @pl.when(chip < 2)
+    def _():
+        kv[2] = jnp.zeros(kv.shape[1:], BF16)
+        docs[2] = jnp.zeros(docs.shape[1:], jnp.int32)
+
+    @pl.when(chip >= n // 2 - 2)
+    def _():
+        recv2[...] = jnp.zeros(recv2.shape, BF16)
+
+    arrived(3)
+    for s in both:
+
+        @pl.when(has_down)
+        def _():
+            doc_up(s, s).wait_recv()
+
+        @pl.when(par == 1)
+        def _():
+            doc_relay(s).start()
 
     arrived(0)
 
     for h in range(HH):
         x = kx[:, h * HD : (h + 1) * HD].astype(F32)
         kv[0, h, 0] = (x * inverse_rms(x) * kgain[...]).astype(BF16)
-        arrived(4 + h)
-
-        @pl.when(has_up)
-        def _():
-            for w in range(2):
-                to_up(h, w).start()
-
-        if h < HH - 1:
-
-            @pl.when(par == 0)
-            def _():
-                for w in range(2):
-                    to_xn(0, h, w).start()
-
-    @pl.when(chip < 2)
-    def _():
-        kv[2] = jnp.zeros(kv.shape[1:], BF16)
-
-    @pl.when(chip >= n // 2 - 2)
-    def _():
-        recv2[...] = jnp.zeros(recv2.shape, BF16)
-
-    @pl.when(has_down)
-    def _():
-        doc_up.wait_recv()
-
-
-    @pl.when(par == 1)
-    def _():
-        doc_xn(2).start()
-
-    doc_xn(0).wait_recv()
+
+    for s in range(2):
+        doc_xn(s, s).wait_recv()
 
     lane = lax.broadcasted_iota(jnp.int32, (1, HD), 1)
     blocks = T // BLK
@@ -190,9 +225,9 @@
                     kd = jnp.where(chip >= slot, docs[slot, m, b : b + 1, :], -1)
                     low = low + jnp.where(kd < qd, BLK, 0)
         lows.append(jnp.maximum(low, lane + (i * HD + 1)))
-    half = len(lows) // 2
+    hl = len(lows) // 2
     low_rows = [
-        jnp.concatenate([x for _ in range(G) for x in lows[t * half : (t + 1) * half]], axis=1)
+        jnp.concatenate([x for _ in range(G) for x in lows[t * hl : (t + 1) * hl]], axis=1)
         for t in range(2)
     ]
     tile_rows = lax.broadcasted_iota(jnp.int32, (T, G * T), 0)
@@ -200,20 +235,25 @@
     causal = tile_rows <= lax.rem(tile_cols, T)
 
     arrived(1)
-    arrived(2)
+    for h in range(HH):
+        arrived(4 + h)
 
     def key_tile(h, which, b):
         slot, r = 2 - b // 2, b % 2
+        if which == 0 and slot > 0:
+            return kn[slot - 1, r * T : (r + 1) * T, :]
         return kv[slot, h, which, r * T : (r + 1) * T, :]
 
     def take_up(h, w):
-        @pl.when(has_down)
-        def _():
-            to_up(h, w).wait_recv()
-
-        @pl.when(par == 1)
-        def _():
-            to_xn(2, h, w).start()
+        for s in both:
+
+            @pl.when(has_down)
+            def _():
+                to_up(h, w, s, s).wait_recv()
+
+            @pl.when(par == 1)
+            def _():
+                relay(h, w, s).start()
 
     def g1(h, w):
         return remote(
@@ -225,15 +265,13 @@
             send2.at[h, w], recv2.at[h, w], g2_send.at[h, w], g2_recv.at[h, w], down
         )
 
-    def pass_down(h):
-        for w in range(2):
+    def pass_down(h, w):
+        @pl.when(par == 1)
+        def _():
             g1(h, w).wait_recv()
-
-            @pl.when(par == 1)
-            def _():
-                send2[h, w] = (part2[h, w] + recv1[h, w].astype(F32)).astype(BF16)
-
-            @pl.when((par == 1) & has_down)
+            send2[h, w] = (part2[h, w] + recv1[h, w].astype(F32)).astype(BF16)
+
+            @pl.when(has_down)
             def _():
                 g2(h, w).start()
 
@@ -306,17 +344,22 @@
 
         for w in range(2):
 
-            @pl.when(h == HH - 2 + w)
+            @pl.when(h == 2 * w)
             def _():
                 take_up(0, w)
 
         return carry
 
     lax.fori_loop(0, HH, own_forward, 0)
+    arrived(2)
 
     def head(h, carry):
         for w in range(2):
-            to_xn(0, h, w).wait_recv()
+            for s in range(2):
+                relay(h, w, s).wait_recv()
+        for slot in (1, 2):
+            x = kv[slot, h, 0].astype(F32)
+            kn[slot - 1] = (x * inverse_rms(x) * kgain[...]).astype(BF16)
         for t in range(2):
             total, o_t = lsum[h, t], osum[h, t]
             for b in range(t, 4):
@@ -341,17 +384,21 @@
             send1[h, 1, at] = dv.astype(BF16)
             for t in terms:
                 dq_t[t] = dq_t[t] + terms[t]
-        for w in range(2):
-            g1(h, w).start()
-
-        @pl.when((par == 0) & (h == 0))
-        def _():
-            for w in range(2):
-                to_xn(0, HH - 1, w).start()
+
+        @pl.when((par == 0) | (h == HH - 1))
+        def _():
+            for w in range(2):
+                g1(h, w).start()
 
         @pl.when(h + 1 < HH)
         def _():
             take_up(h + 1, 1)
+
+        @pl.when((par == 1) & (h == HH - 2))
+        def _():
+            for i in range(HH - 1):
+                for w in range(2):
+                    g1(i, w).start()
 
         for b in (0, 1):
             dk, dv, terms = backward(h, b, {t: efar[t, b] for t in range(b + 1)})
@@ -367,11 +414,22 @@
         def _():
             for w in range(2):
                 send2[h, w] = part2[h, w].astype(BF16)
-                g2(h, w).start()
-
-        @pl.when(h > 1)
-        def _():
-            pass_down(h - 2)
+
+            @pl.when(h == HH - 2)
+            def _():
+                for i in range(HH - 1):
+                    for w in range(2):
+                        g2(i, w).start()
+
+            @pl.when(h == HH - 1)
+            def _():
+                for w in range(2):
+                    g2(h, w).start()
+
+        @pl.when(h == HH - 1)
+        def _():
+            for w in range(2):
+                pass_down(0, w)
 
         return carry
 
@@ -399,14 +457,18 @@
         far.start()
         near.start()
 
-        @pl.when(h == 1)
-        def _():
-            pass_down(HH - 2)
+        for w in range(2):
+
+            @pl.when(h == 1 + w)
+            def _():
+                pass_down(1, w)
 
         return carry
 
     lax.fori_loop(0, HH, own_backward, 0)
-    pass_down(HH - 1)
+    for i in range(2, HH):
+        for w in range(2):
+            pass_down(i, w)
 
     def finish(h, carry):
         cols = pl.ds(pl.multiple_of(h * HD, HD), HD)
@@ -414,6 +476,11 @@
         def _():
             for w in range(2):
                 g2(h, w).wait_recv()
+
+        @pl.when(par == 0)
+        def _():
+            for w in range(2):
+                g1(h, w).wait_recv()
 
         own = part0[h] + recv2[h].astype(F32)
         own = own + jnp.where(par == 0, recv1[h].astype(F32), 0.0)
@@ -433,21 +500,24 @@
     for rc, lc in swaps:
         rc.wait_send()
 
-    @pl.when(has_up)
-    def _():
-        doc_up.wait_send()
-
-    doc_xn(0).wait_send()
+    for s in range(2):
+        doc_xn(s, s).wait_send()
+
+        @pl.when(has_up)
+        def _():
+            doc_up(s, s).wait_send()
 
     def drain(h, carry):
         for w in range(2):
-            to_xn(0, h, w).wait_send()
+            for s in range(2):
+                to_xn(h, w, s, s).wait_send()
             g1(h, w).wait_send()
 
         @pl.when(has_up)
         def _():
             for w in range(2):
-                to_up(h, w).wait_send()
+                for s in range(2):
+                    to_up(h, w, s, s).wait_send()
 
         @pl.when(has_down)
         def _():
@@ -481,6 +551,7 @@
         pltpu.VMEM(doc_tile, jnp.int32),
         pltpu.VMEM((3, 2) + doc_tile, jnp.int32),
         pltpu.VMEM((3, HH, 2, C, HD), BF16),
+        pltpu.VMEM((2, C, HD), BF16),
         pltpu.VMEM((2, per - 1, T, G * T), BF16),
         pltpu.VMEM((HH, 3, T, G * T), BF16),
         pltpu.VMEM((HH, 2, G * T, HD), BF16),
@@ -497,8 +568,8 @@
         pltpu.VMEM((HH, 2, C, HD), BF16),
         pltpu.VMEM((2, T, HH * G * HD), BF16),
         pltpu.VMEM((2, 2, T, HH * HD), BF16),
-        DMA((5 + HH,)), DMA((5 + HH,)), DMA((5 + HH,)), DMA((4,)),
-        DMA((HH, 2)), DMA((HH, 2)), DMA((HH, 2)), DMA((HH, 2)),
+        DMA((4 + HH,)), DMA((4 + HH,)), DMA((4 + HH,)), DMA((2,)), DMA((2,)), DMA((2,)), DMA((2,)),
+        DMA((HH, 2, 2)), DMA((HH, 2, 2)), DMA((HH, 2, 2)), DMA((HH, 2, 2)),
         DMA((HH, 2)), DMA((HH, 2)), DMA((HH, 2)), DMA((HH, 2)),
         DMA((HH,)), DMA((HH,)), DMA((HH,)), DMA((2, HH)), DMA((2, HH)), DMA((2, HH)),
     ]

time: 75 us -> 66.7 us (0.89)
  Pallas kernels: 71.6 us -> 63.3 us
    pallas_call x1, Pallas kernels: 71.6 us -> 63.3 us  [on_device(): pl.pallas_call(functools.partial(kernel, n), out_shape=(pltpu.VMEM(querie...]
where the time goes in v1:
time: 66.7 us; the launch traced here: 66.5 us
  Pallas kernels  63.3 us (95%)
  local copies, waits for them, and re-layouts  2.56 us (4%)
    pallas_call x1, Pallas kernels, on_device(): pl.pallas_call(functools.partial(kernel, n), out_shape=(pltpu.VMEM(querie...  63.3 us
    unnamed x3, local copies, waits for them, and re-layouts  2.56 us

profile of v1, /device:TPU:3, one launch (start us, length us, event | category | flops | bytes accessed | tf_op | source)
XLA Modules:
  0.0 66.5 jit_solution(14906907849970801499)
XLA Ops:
  0.6 63.3 %shard_map.94 = (bf16[256,2048]{1,0:T(8,128)(2,1)S(1)}, bf16[256,1024]{1,0:T(8,128)(2,1)S(1)}, bf16[256,1024]{1,0:T(8,128)(2,1)S(1)}) custom-call(bf16[256,2048]{1,0:T(8,128)(2,1)} %q_in.1, bf16[256,1024]{1,0:T(8,128)(2,1)} %k_in.1, bf16[256,1024]{1,0:T(8,128)(2,1)} %v_in.1, bf16[256,2048]{1,0:T(8,128)(2,1)} %g_in.1, f32[1,128]{1,0:T(1,128)} %bitcast.2, ...), custom_call_target="tpu_custom_call" | custom-call | tf_op jit(solution)/shard_map/pallas_call | solution.py:576
  64.0 1.0 %copy.13 = bf16[256,2048]{1,0:T(8,128)(2,1)} copy(bf16[256,2048]{1,0:T(8,128)(2,1)S(1)} %get-tuple-element.3) | data formatting | bytes 2097152
  65.0 0.8 %copy.14 = bf16[256,1024]{1,0:T(8,128)(2,1)} copy(bf16[256,1024]{1,0:T(8,128)(2,1)S(1)} %get-tuple-element.4) | data formatting | bytes 1048576
  65.8 0.8 %copy.15 = bf16[256,1024]{1,0:T(8,128)(2,1)} copy(bf16[256,1024]{1,0:T(8,128)(2,1)S(1)} %get-tuple-element.5) | data formatting | bytes 1048576

commit v2 on v1

--- a/solution.py
+++ b/solution.py
@@ -64,10 +64,22 @@
 
     barrier = pltpu.get_barrier_semaphore()
     flip = 1 - 2 * core
-    for who in (partner, xn, xn + flip, up, up + flip, down, down + flip):
-        pl.semaphore_signal(
-            barrier, inc=1, device_id={"ctx": who}, device_id_type=pl.DeviceIdType.MESH
-        )
+
+    def greet(*peers):
+        for who in peers:
+            pl.semaphore_signal(
+                barrier, inc=1, device_id={"ctx": who}, device_id_type=pl.DeviceIdType.MESH
+            )
+
+    @pl.when(has_up)
+    def _():
+        greet(up, up + flip)
+
+    @pl.when(has_down)
+    def _():
+        greet(down, down + flip)
+
+    greet(xn, xn + flip, partner)
 
     def remote(src, dst, s, r, who):
         return pltpu.make_async_remote_copy(
@@ -147,7 +159,7 @@
     for i in order:
         swaps[i][1].start()
 
-    pl.semaphore_wait(barrier, 7)
+    pl.semaphore_wait(barrier, 3 + 2 * jnp.where(has_up, 1, 0) + 2 * jnp.where(has_down, 1, 0))
 
     both = (core, other)
     swaps[3][0].start()
@@ -170,11 +182,13 @@
                 for j in both:
                     to_up(h, w, j, core).start()
 
-        @pl.when(par == 0)
-        def _():
-            for w in range(2):
-                for j in both:
-                    to_xn(h, w, j, core).start()
+        if h < HH - 1:
+
+            @pl.when(par == 0)
+            def _():
+                for w in range(2):
+                    for j in both:
+                        to_xn(h, w, j, core).start()
 
     for i in order[1:]:
         swaps[i][0].start()
@@ -199,6 +213,18 @@
         def _():
             doc_relay(s).start()
 
+    def take_up(h, w, *sides):
+        @pl.when(par == 1)
+        def _():
+            for s in sides:
+
+                @pl.when(has_down)
+                def _():
+                    to_up(h, w, s, s).wait_recv()
+
+                relay(h, w, s).start()
+
+    take_up(0, 0, core)
     arrived(0)
 
     for h in range(HH):
@@ -244,36 +270,37 @@
             return kn[slot - 1, r * T : (r + 1) * T, :]
         return kv[slot, h, which, r * T : (r + 1) * T, :]
 
-    def take_up(h, w):
-        for s in both:
-
-            @pl.when(has_down)
-            def _():
-                to_up(h, w, s, s).wait_recv()
-
-            @pl.when(par == 1)
-            def _():
-                relay(h, w, s).start()
-
-    def g1(h, w):
+    away = (other, core)
+
+    def g1(h, w, m):
         return remote(
-            send1.at[h, w], recv1.at[h, w], g1_send.at[h, w], g1_recv.at[h, w], xn
-        )
-
-    def g2(h, w):
+            send1.at[h, w, half(m)], recv1.at[h, w, half(m)],
+            g1_send.at[h, w, m], g1_recv.at[h, w, m], xn,
+        )
+
+    def g2(h, w, m):
         return remote(
-            send2.at[h, w], recv2.at[h, w], g2_send.at[h, w], g2_recv.at[h, w], down
-        )
+            send2.at[h, w, half(m)], recv2.at[h, w, half(m)],
+            g2_send.at[h, w, m], g2_recv.at[h, w, m], down,
+        )
+
+    def start_all(copy, *heads):
+        for h in heads:
+            for w in range(2):
+                for m in away:
+                    copy(h, w, m).start()
 
     def pass_down(h, w):
         @pl.when(par == 1)
         def _():
-            g1(h, w).wait_recv()
-            send2[h, w] = (part2[h, w] + recv1[h, w].astype(F32)).astype(BF16)
-
-            @pl.when(has_down)
-            def _():
-                g2(h, w).start()
+            for m in away:
+                g1(h, w, m).wait_recv()
+                total = part2[h, w, half(m)] + recv1[h, w, half(m)].astype(F32)
+                send2[h, w, half(m)] = total.astype(BF16)
+
+                @pl.when(has_down)
+                def _():
+                    g2(h, w, m).start()
 
     def fq(h):
         cols = pl.ds(pl.multiple_of(h * (G * HD), G * HD), G * HD)
@@ -283,17 +310,20 @@
             pltpu.make_async_copy(dq.at[core, :, cols], out_q.at[:, to], fq_local.at[h]),
         )
 
-    def fk(h):
+    def fk_far(w, h):
         cols = pl.ds(pl.multiple_of(h * HD, HD), HD)
         to = pl.ds(pl.multiple_of(core * KW + h * HD, HD), HD)
-        pairs = []
-        for w, out in ((0, out_k), (1, out_v)):
-            pairs.append((
-                remote(dkv.at[w, other, :, cols], out.at[:, to], fk_send.at[w, h],
-                       fk_recv.at[w, h], partner),
-                pltpu.make_async_copy(dkv.at[w, core, :, cols], out.at[:, to], fk_local.at[w, h]),
-            ))
-        return pairs
+        return remote(
+            dkv.at[w, other, :, cols], (out_k, out_v)[w].at[:, to],
+            fk_send.at[w, h], fk_recv.at[w, h], partner,
+        )
+
+    def fk_near(w, h):
+        cols = pl.ds(pl.multiple_of(h * HD, HD), HD)
+        to = pl.ds(pl.multiple_of(core * KW + h * HD, HD), HD)
+        return pltpu.make_async_copy(
+            dkv.at[w, core, :, cols], (out_k, out_v)[w].at[:, to], fk_local.at[w, h]
+        )
 
     qg = qgain[...] * qk_scale
     own_at = {(0, 4): 0, (1, 4): 1, (1, 5): 2}
@@ -342,11 +372,11 @@
             lsum[h, t] = total
             osum[h, t] = o_t
 
-        for w in range(2):
-
-            @pl.when(h == 2 * w)
+        for i, at in enumerate(((0, other), (1, core), (1, other))):
+
+            @pl.when(h == i)
             def _():
-                take_up(0, w)
+                take_up(0, *at)
 
         return carry
 
@@ -354,6 +384,17 @@
     arrived(2)
 
     def head(h, carry):
+        @pl.when((par == 0) & has_down)
+        def _():
+            for w in range(2):
+                for s in range(2):
+                    to_up(h, w, s, s).wait_recv()
+
+        @pl.when(h == HH - 1)
+        def _():
+            for w in range(2):
+                pass_down(0, w)
+
         for w in range(2):
             for s in range(2):
                 relay(h, w, s).wait_recv()
@@ -372,9 +413,19 @@
             drow[h, t] = jnp.sum(g_t.astype(BF16).astype(F32) * o_t, axis=0, keepdims=True) * inv
             gn[h, t] = g_t.T.astype(BF16)
 
+            if t == 0:
+
+                @pl.when(h + 1 < HH)
+                def _():
+                    take_up(h + 1, 0, core)
+
         @pl.when(h + 1 < HH)
         def _():
-            take_up(h + 1, 0)
+            take_up(h + 1, 0, other)
+
+        @pl.when((par == 0) & has_down & (h == HH - 2))
+        def _():
+            start_all(g2, *range(HH - 2))
 
         dq_t = [0.0, 0.0]
         for b in (2, 3):
@@ -387,18 +438,21 @@
 
         @pl.when((par == 0) | (h == HH - 1))
         def _():
-            for w in range(2):
-                g1(h, w).start()
+            start_all(g1, h)
+
+        @pl.when((par == 0) & (h == 0))
+        def _():
+            for w in range(2):
+                for j in both:
+                    to_xn(HH - 1, w, j, core).start()
+
+        @pl.when(h == HH - 1)
+        def _():
+            pass_down(1, 0)
 
         @pl.when(h + 1 < HH)
         def _():
-            take_up(h + 1, 1)
-
-        @pl.when((par == 1) & (h == HH - 2))
-        def _():
-            for i in range(HH - 1):
-                for w in range(2):
-                    g1(i, w).start()
+            take_up(h + 1, 1, core)
 
         for b in (0, 1):
             dk, dv, terms = backward(h, b, {t: efar[t, b] for t in range(b + 1)})
@@ -415,21 +469,19 @@
             for w in range(2):
                 send2[h, w] = part2[h, w].astype(BF16)
 
-            @pl.when(h == HH - 2)
+            @pl.when(h >= HH - 2)
             def _():
-                for i in range(HH - 1):
-                    for w in range(2):
-                        g2(i, w).start()
-
-            @pl.when(h == HH - 1)
+                start_all(g2, h)
+
+        @pl.when(h + 1 < HH)
+        def _():
+            take_up(h + 1, 1, other)
+
+        for at, ready in ((HH - 3, range(HH - 3)), (HH - 2, range(HH - 3, HH - 1))):
+
+            @pl.when((par == 1) & (h == at))
             def _():
-                for w in range(2):
-                    g2(h, w).start()
-
-        @pl.when(h == HH - 1)
-        def _():
-            for w in range(2):
-                pass_down(0, w)
+                start_all(g1, *ready)
 
         return carry
 
@@ -457,42 +509,40 @@
         far.start()
         near.start()
 
-        for w in range(2):
-
-            @pl.when(h == 1 + w)
+        for i, at in ((0, (1, 1)), (2, (2, 0))):
+
+            @pl.when(h == i)
             def _():
-                pass_down(1, w)
+                pass_down(*at)
 
         return carry
 
     lax.fori_loop(0, HH, own_backward, 0)
-    for i in range(2, HH):
+    pass_down(2, 1)
+    for i in range(3, HH):
         for w in range(2):
             pass_down(i, w)
 
     def finish(h, carry):
         cols = pl.ds(pl.multiple_of(h * HD, HD), HD)
-        @pl.when(has_up)
-        def _():
-            for w in range(2):
-                g2(h, w).wait_recv()
-
-        @pl.when(par == 0)
-        def _():
-            for w in range(2):
-                g1(h, w).wait_recv()
-
-        own = part0[h] + recv2[h].astype(F32)
-        own = own + jnp.where(par == 0, recv1[h].astype(F32), 0.0)
-        x = kx[:, cols].astype(F32)
-        dk = norm_back(x, inverse_rms(x), kgain[...], own[0]).astype(BF16)
-        dv = own[1].astype(BF16)
-        for m in range(2):
-            dkv[0, m, :, cols] = dk[m * T : (m + 1) * T]
-            dkv[1, m, :, cols] = dv[m * T : (m + 1) * T]
-        for far, near in fk(h):
-            far.start()
-            near.start()
+        for w in range(2):
+            for m, out in ((other, fk_far), (core, fk_near)):
+
+                @pl.when(has_up)
+                def _():
+                    g2(h, w, m).wait_recv()
+
+                @pl.when(par == 0)
+                def _():
+                    g1(h, w, m).wait_recv()
+
+                d = part0[h, w, half(m)] + recv2[h, w, half(m)].astype(F32)
+                d = d + jnp.where(par == 0, recv1[h, w, half(m)].astype(F32), 0.0)
+                if w == 0:
+                    x = kx[half(m), cols].astype(F32)
+                    d = norm_back(x, inverse_rms(x), kgain[...], d)
+                dkv[w, m, :, cols] = d.astype(BF16)
+                out(w, h).start()
         return carry
 
     lax.fori_loop(0, HH, finish, 0)
@@ -511,7 +561,7 @@
         for w in range(2):
             for s in range(2):
                 to_xn(h, w, s, s).wait_send()
-            g1(h, w).wait_send()
+                g1(h, w, s).wait_send()
 
         @pl.when(has_up)
         def _():
@@ -522,9 +572,10 @@
         @pl.when(has_down)
         def _():
             for w in range(2):
-                g2(h, w).wait_send()
-
-        for far, near in [fq(h)] + fk(h):
+                for m in range(2):
+                    g2(h, w, m).wait_send()
+
+        for far, near in (fq(h), (fk_far(0, h), fk_near(0, h)), (fk_far(1, h), fk_near(1, h))):
             far.wait_send()
             far.wait_recv()
             near.wait()
@@ -570,7 +621,7 @@
         pltpu.VMEM((2, 2, T, HH * HD), BF16),
         DMA((4 + HH,)), DMA((4 + HH,)), DMA((4 + HH,)), DMA((2,)), DMA((2,)), DMA((2,)), DMA((2,)),
         DMA((HH, 2, 2)), DMA((HH, 2, 2)), DMA((HH, 2, 2)), DMA((HH, 2, 2)),
-        DMA((HH, 2)), DMA((HH, 2)), DMA((HH, 2)), DMA((HH, 2)),
+        DMA((HH, 2, 2)), DMA((HH, 2, 2)), DMA((HH, 2, 2)), DMA((HH, 2, 2)),
         DMA((HH,)), DMA((HH,)), DMA((HH,)), DMA((2, HH)), DMA((2, HH)), DMA((2, HH)),
     ]
     return pl.pallas_call(

time: 66.7 us -> 60.9 us (0.913)
  Pallas kernels: 63.3 us -> 57.4 us
    pallas_call x1, Pallas kernels: 63.3 us -> 57.4 us  [on_device(): pl.pallas_call(functools.partial(kernel, n), out_shape=(pltpu.VMEM(querie...]
where the time goes in v2:
time: 60.9 us; the launch traced here: 60.6 us
  Pallas kernels  57.4 us (94%)
  local copies, waits for them, and re-layouts  2.56 us (4%)
  between operations  0.64 us (1%)
    pallas_call x1, Pallas kernels, on_device(): pl.pallas_call(functools.partial(kernel, n), out_shape=(pltpu.VMEM(querie...  57.4 us
    unnamed x3, local copies, waits for them, and re-layouts  2.56 us

profile of v2, /device:TPU:3, one launch (start us, length us, event | category | flops | bytes accessed | tf_op | source)
XLA Modules:
  0.0 60.6 jit_solution(14081824573366359033)
XLA Ops:
  0.6 57.4 %shard_map.94 = (bf16[256,2048]{1,0:T(8,128)(2,1)S(1)}, bf16[256,1024]{1,0:T(8,128)(2,1)S(1)}, bf16[256,1024]{1,0:T(8,128)(2,1)S(1)}) custom-call(bf16[256,2048]{1,0:T(8,128)(2,1)} %q_in.1, bf16[256,1024]{1,0:T(8,128)(2,1)} %k_in.1, bf16[256,1024]{1,0:T(8,128)(2,1)} %v_in.1, bf16[256,2048]{1,0:T(8,128)(2,1)} %g_in.1, f32[1,128]{1,0:T(1,128)} %bitcast.2, ...), custom_call_target="tpu_custom_call" | custom-call | tf_op jit(solution)/shard_map/pallas_call | solution.py:627
  58.1 1.0 %copy.13 = bf16[256,2048]{1,0:T(8,128)(2,1)} copy(bf16[256,2048]{1,0:T(8,128)(2,1)S(1)} %get-tuple-element.3) | data formatting | bytes 2097152
  59.0 0.8 %copy.14 = bf16[256,1024]{1,0:T(8,128)(2,1)} copy(bf16[256,1024]{1,0:T(8,128)(2,1)S(1)} %get-tuple-element.4) | data formatting | bytes 1048576
  59.8 0.8 %copy.15 = bf16[256,1024]{1,0:T(8,128)(2,1)} copy(bf16[256,1024]{1,0:T(8,128)(2,1)S(1)} %get-tuple-element.5) | data formatting | bytes 1048576

commit v3 on v2

--- a/solution.py
+++ b/solution.py
@@ -582,6 +582,17 @@
         return carry
 
     lax.fori_loop(0, HH, drain, 0)
+
+
+def put_out(a, b, c, out_a, out_b, out_c, sems):
+    copies = [
+        pltpu.make_async_copy(src, dst, sems.at[i])
+        for i, (src, dst) in enumerate(((a, out_a), (b, out_b), (c, out_c)))
+    ]
+    for copy in copies:
+        copy.start()
+    for copy in copies:
+        copy.wait()
 
 
 def on_device(n, queries, keys, values, out_grad, q_gain, k_gain, doc_ids):
@@ -624,7 +635,7 @@
         DMA((HH, 2, 2)), DMA((HH, 2, 2)), DMA((HH, 2, 2)), DMA((HH, 2, 2)),
         DMA((HH,)), DMA((HH,)), DMA((HH,)), DMA((2, HH)), DMA((2, HH)), DMA((2, HH)),
     ]
-    return pl.pallas_call(
+    grads = pl.pallas_call(
         functools.partial(kernel, n),
         out_shape=(
             pltpu.VMEM(queries.shape, BF16),
@@ -638,6 +649,14 @@
             collective_id=0, has_side_effects=True, vmem_limit_bytes=64700000
         ),
     )(queries, keys, values, out_grad, q_gain.reshape(1, HD), k_gain.reshape(1, HD), doc_ids)
+    return pl.pallas_call(
+        put_out,
+        out_shape=tuple(jax.ShapeDtypeStruct(x.shape, BF16) for x in (queries, keys, values)),
+        in_specs=[pl.BlockSpec(memory_space=pl.ANY)] * 3,
+        out_specs=(anywhere, anywhere, anywhere),
+        scratch_shapes=[DMA((3,))],
+        compiler_params=pltpu.CompilerParams(vmem_limit_bytes=1 << 20),
+    )(*grads)
 
 
 def solution(mesh):

time: 60.9 us -> 59.6 us (0.979)
  local copies, waits for them, and re-layouts: 2.56 us -> 0 us
  Pallas kernels: 57.4 us -> 58.8 us
    unnamed x3 -> x0, local copies, waits for them, and re-layouts: 2.56 us -> none
    pallas_call x0 -> x1, Pallas kernels: none -> 1.34 us  [on_device(): pl.pallas_call(put_out, out_shape=tuple((jax.ShapeDtypeStruct(x.shape, BF...]
where the time goes in v3:
time: 59.6 us; the launch traced here: 59.4 us
  Pallas kernels  58.8 us (99%)
  between operations  0.64 us (1%)
    pallas_call x1, Pallas kernels, on_device(): pl.pallas_call(functools.partial(kernel, n), out_shape=(pltpu.VMEM(querie...  57.4 us
    pallas_call x1, Pallas kernels, on_device(): pl.pallas_call(put_out, out_shape=tuple((jax.ShapeDtypeStruct(x.shape, BF...  1.34 us

profile of v3, /device:TPU:3, one launch (start us, length us, event | category | flops | bytes accessed | tf_op | source)
XLA Modules:
  0.0 59.4 jit_solution(3118383498617123214)
XLA Ops:
  0.6 57.4 %shard_map.94 = (bf16[256,2048]{1,0:T(8,128)(2,1)S(1)}, bf16[256,1024]{1,0:T(8,128)(2,1)S(1)}, bf16[256,1024]{1,0:T(8,128)(2,1)S(1)}) custom-call(bf16[256,2048]{1,0:T(8,128)(2,1)} %q_in.1, bf16[256,1024]{1,0:T(8,128)(2,1)} %k_in.1, bf16[256,1024]{1,0:T(8,128)(2,1)} %v_in.1, bf16[256,2048]{1,0:T(8,128)(2,1)} %g_in.1, f32[1,128]{1,0:T(1,128)} %bitcast.2, ...), custom_call_target="tpu_custom_call" | custom-call | tf_op jit(solution)/shard_map/pallas_call | solution.py:638
  58.1 1.3 %shard_map.95 = (bf16[256,2048]{1,0:T(8,128)(2,1)}, bf16[256,1024]{1,0:T(8,128)(2,1)}, bf16[256,1024]{1,0:T(8,128)(2,1)}) custom-call(bf16[256,2048]{1,0:T(8,128)(2,1)S(1)} %get-tuple-element.6.a, bf16[256,1024]{1,0:T(8,128)(2,1)S(1)} %get-tuple-element.7.b, bf16[256,1024]{1,0:T(8,128)(2,1)S(1)} %get-tuple-element.8.c), custom_call_target="tpu_custom_call" | custom-call | tf_op jit(solution)/shard_map/pallas_call | solution.py:652
